TPU v7x, 32 devices: a whole 2x2x4 slice. The times are simulated.
32 devices in a mesh: seq: 8 (over z, y), mp: 4 (over x, core).
Axes of the slice: x: 2, y: 2, z: 4, core: 2. Of those that a mesh axis runs over, the one named last changes fastest.
Arguments:
- tokens: bfloat16 [4096, 768], P('seq'), may hold values from -6 to 6
- item_lengths: int32 [8], replicated, may hold values from 1 to 2048, 4096 in all
- w_qkv: bfloat16 [3, 768, 768], P(None, None, 'mp'), may hold values from -2 to 2
- b_qv: float32 [2, 768], P(None, 'mp'), may hold values from -2 to 2
- taps: float32 [12, 33], P('mp'), may hold values from -0.072 to 0.072
- w_out: bfloat16 [768, 768], P('mp'), may hold values from -1.75 to 1.75
- b_out: float32 [768], replicated, may hold values from -3 to 3
- ln1_gain: float32 [768], replicated, may hold values from 0.5 to 1.5
- ln1_bias: float32 [768], replicated, may hold values from -2 to 2
- w_up: bfloat16 [768, 3072], P(None, 'mp'), may hold values from -0.21875 to 0.21875
- b_up: float32 [3072], P('mp'), may hold values from -3 to 3
- w_down: bfloat16 [3072, 768], P('mp'), may hold values from -0.109375 to 0.109375
- b_down: float32 [768], replicated, may hold values from -3 to 3
- ln2_gain: float32 [768], replicated, may hold values from 0.5 to 1.5
- ln2_bias: float32 [768], replicated, may hold values from -2 to 2
- d_out: bfloat16 [4096, 768], P('seq'), may hold values from -6 to 6
Outputs:
- layer_output: bfloat16 [4096, 768], P('seq')
- d_tokens: bfloat16 [4096, 768], P('seq')
- d_w_qkv: float32 [3, 768, 768], P(None, None, 'mp')
- d_b_qv: float32 [2, 768], P(None, 'mp')
- d_taps: float32 [12, 33], P('mp')
- d_w_out: float32 [768, 768], P('mp')
- d_b_out: float32 [768], replicated
- d_ln1_gain: float32 [768], replicated
- d_ln1_bias: float32 [768], replicated
- d_w_up: float32 [768, 3072], P(None, 'mp')
- d_b_up: float32 [3072], P('mp')
- d_w_down: float32 [3072, 768], P('mp')
- d_b_down: float32 [768], replicated
- d_ln2_gain: float32 [768], replicated
- d_ln2_bias: float32 [768], replicated
Inputs may be any that keep to these rules, and one draw needn't show every extreme that they name: `item_lengths`: the lengths sum to 4096; the largest is exactly 2048, and no item is longer than 4096.
All inputs are finite; a program needn't handle non-finite values.
Results may differ from a plain program's by a relative error of at most 0.017.
Values may be sent and summed in bfloat16 or wider, within the bound.
No kernel may reach another device: no remote copies, remote signals or barrier semaphores. Data moves between devices by JAX's collectives and lax.ppermute only.
A program may use at most 192 MiB of HBM per device.

v0:
```python
import math
import jax
import jax.numpy as jnp
from jax import lax
from jax.sharding import PartitionSpec as P

SHRINK = 0.95
NORM_EPS = 1e-06
LAYER_EPS = 1e-05


def padded(cells, sides, width):
    for axis, dim in sides:
        count = lax.axis_size(axis)
        ends = count - 1
        head = lax.slice_in_dim(cells, 0, width, axis=dim)
        tail = lax.slice_in_dim(cells, cells.shape[dim] - width, cells.shape[dim], axis=dim)
        cells = jnp.concatenate(
            [
                lax.ppermute(tail, axis, [(i, (i + 1) % count) for i in range(ends)]),
                cells,
                lax.ppermute(head, axis, [((i + 1) % count, i) for i in range(ends)]),
            ],
            axis=dim,
        )
    return cells


def item_index(positions, ends):
    inside = (positions >= 0) & (positions < ends[-1])
    counted = jnp.sum((positions[:, None] >= ends[None, :]).astype(jnp.int32), axis=1)
    return jnp.where(inside, counted, -1)


def layer_norm(hidden, gain, shift):
    center = hidden - jnp.mean(hidden, axis=-1, keepdims=True)
    scale = lax.rsqrt(jnp.mean(center * center, axis=-1, keepdims=True) + LAYER_EPS)
    normed = center * scale
    return (normed * gain + shift, normed, scale)


def layer_norm_back(grad, normed, scale, gain):
    d_gain = jnp.sum(grad * normed, axis=0)
    d_shift = jnp.sum(grad, axis=0)
    d_normed = grad * gain
    centered = d_normed - jnp.mean(d_normed, axis=-1, keepdims=True)
    d_hidden = scale * (centered - normed * jnp.mean(d_normed * normed, axis=-1, keepdims=True))
    return (d_hidden, d_gain, d_shift)


def block_rows(row_count):
    bound = min(row_count, 1024)
    return max((candidate for candidate in range(1, bound + 1) if row_count % candidate == 0))


def fold_blocks(carry, arrays, start, work):
    row_count = arrays[0].shape[0]
    width = block_rows(row_count)
    stacked = tuple(
        (array.reshape((row_count // width, width) + array.shape[1:]) for array in arrays)
    )
    offsets = start + width * jnp.arange(row_count // width, dtype=jnp.int32)

    def advance(state, inputs):
        return (work(state, inputs[:-1], inputs[-1]), None)

    result, _ = lax.scan(advance, carry, stacked + (offsets,))
    return result


def collision_back(queries, keys_heads, values_heads, d_attn_heads, same):
    scores = jnp.einsum("bhe,khe->hbk", queries, keys_heads, preferred_element_type=jnp.float32)
    cosine = SHRINK * scores
    closeness = 1.0 - jnp.arccos(cosine) / math.pi
    weights = (same[None] * closeness**8).astype(jnp.bfloat16)
    d_weights = jnp.einsum(
        "bhe,khe->hbk", d_attn_heads, values_heads, preferred_element_type=jnp.float32
    )
    slope = same[None] * 8.0 * closeness**7 * SHRINK / (math.pi * jnp.sqrt(1.0 - cosine * cosine))
    d_scores = (d_weights * slope).astype(jnp.bfloat16)
    return (weights, d_scores)


def per_device(
    tokens,
    item_lengths,
    w_qkv,
    b_qv,
    taps,
    w_out,
    b_out,
    ln1_gain,
    ln1_bias,
    w_up,
    b_up,
    w_down,
    b_down,
    ln2_gain,
    ln2_bias,
    d_out,
):
    local_rows = tokens.shape[0]
    heads_here = taps.shape[0]
    kernel = taps.shape[1]
    radius = (kernel - 1) // 2
    columns = w_qkv.shape[2]
    head_size = columns // heads_here
    ends = jnp.cumsum(item_lengths)
    first_row = lax.axis_index("seq") * local_rows
    query_items = item_index(first_row + jnp.arange(local_rows, dtype=jnp.int32), ends)
    rim_items = item_index(
        first_row - radius + jnp.arange(local_rows + 2 * radius, dtype=jnp.int32), ends
    )
    tap_columns = jnp.repeat(taps, head_size, axis=0).T
    bias_rows = jnp.stack([b_qv[0], jnp.zeros_like(b_qv[0]), b_qv[1]])
    projected = (
        jnp.einsum("td,ide->ite", tokens, w_qkv, preferred_element_type=jnp.float32)
        + bias_rows[:, None, :]
    )
    query_raw = projected[0].reshape(local_rows, heads_here, head_size)
    key_raw = projected[1].reshape(local_rows, heads_here, head_size)
    query_scale = lax.rsqrt(jnp.sum(query_raw * query_raw, axis=-1, keepdims=True) + NORM_EPS)
    key_scale = lax.rsqrt(jnp.sum(key_raw * key_raw, axis=-1, keepdims=True) + NORM_EPS)
    query_unit = query_raw * query_scale
    key_unit = key_raw * key_scale
    query_low = query_unit.astype(jnp.bfloat16)
    key_low = key_unit.astype(jnp.bfloat16)
    value_low = projected[2].astype(jnp.bfloat16)
    packed = jnp.concatenate([key_low.reshape(local_rows, columns), value_low], axis=1)
    zero_heads = jnp.zeros((local_rows, heads_here, head_size), jnp.float32)

    def split_pair(block):
        count = block.shape[0]
        first = block[:, :columns].reshape(count, heads_here, head_size)
        second = block[:, columns : 2 * columns].reshape(count, heads_here, head_size)
        return (first, second)

    def attend(state, pieces, offset):
        keys_heads, values_heads = split_pair(pieces[0])
        key_items = item_index(offset + jnp.arange(keys_heads.shape[0], dtype=jnp.int32), ends)
        same = (query_items[:, None] == key_items[None, :]).astype(jnp.float32)
        scores = jnp.einsum(
            "bhe,khe->hbk", query_low, keys_heads, preferred_element_type=jnp.float32
        )
        closeness = 1.0 - jnp.arccos(SHRINK * scores) / math.pi
        weights = (same[None] * closeness**8).astype(jnp.bfloat16)
        return state + jnp.einsum(
            "hbk,khe->bhe", weights, values_heads, preferred_element_type=jnp.float32
        )

    attended = fold_blocks(
        zero_heads, (lax.all_gather(packed, "seq", axis=0, tiled=True),), jnp.int32(0), attend
    )
    attn_scale = lax.rsqrt(jnp.sum(attended * attended, axis=-1, keepdims=True) + NORM_EPS)
    attn_unit = attended * attn_scale
    value_rim = padded(value_low, (("seq", 0),), radius).astype(jnp.float32)
    convolved = jnp.zeros((local_rows, columns), jnp.float32)
    same_list = []
    for shift_at in range(kernel):
        same_rows = (rim_items[shift_at : shift_at + local_rows] == query_items).astype(
            jnp.float32
        )[:, None]
        same_list.append(same_rows)
        convolved = (
            convolved
            + tap_columns[shift_at] * same_rows * value_rim[shift_at : shift_at + local_rows]
        )
    context_low = (attn_unit.reshape(local_rows, columns) + convolved).astype(jnp.bfloat16)
    branch = lax.psum(jnp.dot(context_low, w_out, preferred_element_type=jnp.float32), "mp")
    first_sum = tokens.astype(jnp.float32) + branch + b_out
    first_out, normed_one, scale_one = layer_norm(first_sum, ln1_gain, ln1_bias)
    first_low = first_out.astype(jnp.bfloat16)
    inner = jnp.dot(first_low, w_up, preferred_element_type=jnp.float32) + b_up
    act_low = jax.nn.gelu(inner, approximate=False).astype(jnp.bfloat16)
    mixed = lax.psum(jnp.dot(act_low, w_down, preferred_element_type=jnp.float32), "mp")
    second_sum = first_out + mixed + b_down
    result, normed_two, scale_two = layer_norm(second_sum, ln2_gain, ln2_bias)
    layer_output = result.astype(jnp.bfloat16)
    d_second, d_ln2_gain, d_ln2_bias = layer_norm_back(
        d_out.astype(jnp.float32), normed_two, scale_two, ln2_gain
    )
    d_second_low = d_second.astype(jnp.bfloat16)
    d_b_down = jnp.sum(d_second, axis=0)
    d_w_down = jnp.einsum("tf,td->fd", act_low, d_second_low, preferred_element_type=jnp.float32)
    d_act = jnp.einsum("td,fd->tf", d_second_low, w_down, preferred_element_type=jnp.float32)
    normal_cdf = 0.5 * (1.0 + lax.erf(inner / math.sqrt(2.0)))
    normal_pdf = jnp.exp(-0.5 * inner * inner) / math.sqrt(2.0 * math.pi)
    d_inner_low = (d_act * (normal_cdf + inner * normal_pdf)).astype(jnp.bfloat16)
    d_b_up = jnp.sum(d_inner_low.astype(jnp.float32), axis=0)
    d_w_up = jnp.einsum("td,tf->df", first_low, d_inner_low, preferred_element_type=jnp.float32)
    d_first_part = jnp.einsum("tf,df->td", d_inner_low, w_up, preferred_element_type=jnp.float32)
    d_first_out = d_second + lax.psum(d_first_part, "mp")
    d_first, d_ln1_gain, d_ln1_bias = layer_norm_back(d_first_out, normed_one, scale_one, ln1_gain)
    d_first_low = d_first.astype(jnp.bfloat16)
    d_b_out = jnp.sum(d_first, axis=0)
    d_w_out = jnp.einsum("tc,td->cd", context_low, d_first_low, preferred_element_type=jnp.float32)
    d_context_low = jnp.einsum(
        "td,cd->tc", d_first_low, w_out, preferred_element_type=jnp.float32
    ).astype(jnp.bfloat16)
    d_context = d_context_low.astype(jnp.float32)
    d_context_heads = d_context.reshape(local_rows, heads_here, head_size)
    d_attn = attn_scale * (
        d_context_heads - attn_unit * jnp.sum(attn_unit * d_context_heads, axis=-1, keepdims=True)
    )
    d_attn_low = d_attn.astype(jnp.bfloat16)
    tap_terms = []
    for shift_at in range(kernel):
        summed = jnp.sum(
            d_context * same_list[shift_at] * value_rim[shift_at : shift_at + local_rows], axis=0
        )
        tap_terms.append(jnp.sum(summed.reshape(heads_here, head_size), axis=1))
    d_taps = jnp.stack(tap_terms, axis=1)
    context_rim = padded(d_context_low, (("seq", 0),), radius).astype(jnp.float32)
    d_value_conv = jnp.zeros((local_rows, columns), jnp.float32)
    for shift_at in range(kernel):
        lower = 2 * radius - shift_at
        same_rows = (rim_items[lower : lower + local_rows] == query_items).astype(jnp.float32)[
            :, None
        ]
        d_value_conv = (
            d_value_conv
            + tap_columns[shift_at] * same_rows * context_rim[lower : lower + local_rows]
        )
    value_heads = value_low.reshape(local_rows, heads_here, head_size)
    both_packed = jnp.concatenate(
        [packed, query_low.reshape(local_rows, columns), d_attn_low.reshape(local_rows, columns)],
        axis=1,
    )

    def pair_block(state, pieces, offset):
        d_query, d_keys, d_values = state
        block = pieces[0]
        count = block.shape[0]
        keys_block, values_block = split_pair(block[:, : 2 * columns])
        queries_block, d_attn_block = split_pair(block[:, 2 * columns :])
        other_items = item_index(offset + jnp.arange(count, dtype=jnp.int32), ends)
        same = (query_items[:, None] == other_items[None, :]).astype(jnp.float32)
        weights, d_scores = collision_back(query_low, keys_block, values_block, d_attn_low, same)
        d_query = d_query + jnp.einsum(
            "hbk,khe->bhe", d_scores, keys_block, preferred_element_type=jnp.float32
        )
        weights_own, d_scores_own = collision_back(
            queries_block, key_low, value_heads, d_attn_block, same.T
        )
        d_keys = d_keys + jnp.einsum(
            "hbk,bhe->khe", d_scores_own, queries_block, preferred_element_type=jnp.float32
        )
        d_values = d_values + jnp.einsum(
            "hbk,bhe->khe", weights_own, d_attn_block, preferred_element_type=jnp.float32
        )
        return (d_query, d_keys, d_values)

    zero_state = (zero_heads, zero_heads, zero_heads)
    d_query, d_key_unit, d_value_heads = fold_blocks(
        zero_state,
        (lax.all_gather(both_packed, "seq", axis=0, tiled=True),),
        jnp.int32(0),
        pair_block,
    )
    d_value_attn = d_value_heads.reshape(local_rows, columns)
    d_query_raw = query_scale * (
        d_query - query_unit * jnp.sum(query_unit * d_query, axis=-1, keepdims=True)
    )
    d_key_raw = key_scale * (
        d_key_unit - key_unit * jnp.sum(key_unit * d_key_unit, axis=-1, keepdims=True)
    )
    d_value = d_value_attn + d_value_conv
    d_projected_low = jnp.stack(
        [d_query_raw.reshape(local_rows, columns), d_key_raw.reshape(local_rows, columns), d_value]
    ).astype(jnp.bfloat16)
    d_bias_all = jnp.sum(d_projected_low.astype(jnp.float32), axis=1)
    d_b_qv = jnp.stack([d_bias_all[0], d_bias_all[2]])
    d_w_qkv = jnp.einsum("td,ite->ide", tokens, d_projected_low, preferred_element_type=jnp.float32)
    d_tokens_part = jnp.einsum(
        "ite,ide->td", d_projected_low, w_qkv, preferred_element_type=jnp.float32
    )
    d_tokens = (
        d_first + lax.psum(d_tokens_part.astype(jnp.bfloat16), "mp").astype(jnp.float32)
    ).astype(jnp.bfloat16)
    summed_grads = (
        lax.psum(d_w_qkv.astype(jnp.bfloat16), "seq").astype(jnp.float32),
        lax.psum(d_b_qv.astype(jnp.bfloat16), "seq").astype(jnp.float32),
        lax.psum(d_taps.astype(jnp.bfloat16), "seq").astype(jnp.float32),
        lax.psum(d_w_out.astype(jnp.bfloat16), "seq").astype(jnp.float32),
        lax.psum(d_b_out.astype(jnp.bfloat16), "seq").astype(jnp.float32),
        lax.psum(d_ln1_gain.astype(jnp.bfloat16), "seq").astype(jnp.float32),
        lax.psum(d_ln1_bias.astype(jnp.bfloat16), "seq").astype(jnp.float32),
        lax.psum(d_w_up.astype(jnp.bfloat16), "seq").astype(jnp.float32),
        lax.psum(d_b_up.astype(jnp.bfloat16), "seq").astype(jnp.float32),
        lax.psum(d_w_down.astype(jnp.bfloat16), "seq").astype(jnp.float32),
        lax.psum(d_b_down.astype(jnp.bfloat16), "seq").astype(jnp.float32),
        lax.psum(d_ln2_gain.astype(jnp.bfloat16), "seq").astype(jnp.float32),
        lax.psum(d_ln2_bias.astype(jnp.bfloat16), "seq").astype(jnp.float32),
    )
    return (layer_output, d_tokens) + tuple(summed_grads)


def solution(mesh):
    placed = (
        P("seq", None),
        P(),
        P(None, None, "mp"),
        P(None, "mp"),
        P("mp", None),
        P("mp", None),
        P(),
        P(),
        P(),
        P(None, "mp"),
        P("mp"),
        P("mp", None),
        P(),
        P(),
        P(),
        P("seq", None),
    )
    return jax.shard_map(
        per_device,
        mesh=mesh,
        in_specs=placed,
        out_specs=(
            P("seq", None),
            P("seq", None),
            P(None, None, "mp"),
            P(None, "mp"),
            P("mp", None),
            P("mp", None),
            P(),
            P(),
            P(),
            P(None, "mp"),
            P("mp"),
            P("mp", None),
            P(),
            P(),
            P(),
        ),
        check_vma=False,
    )
```

profile of v0, /device:TPU:0, one launch (start us, length us, event | category | flops | bytes accessed | tf_op | source)
XLA Modules:
  0.0 956.8 jit_solution(4926142767283352020)
XLA Ops:
  14.3 4.9 collective-permute-start
  26.7 52.4 %all-gather.3.cloned.1.call-done = bf16[4096,384]{0,1:T(8,128)(2,1)} async-done(((bf16[512,384]{0,1:T(8,128)(2,1)}), bf16[4096,384]{0,1:T(8,128)(2,1)}) %all-gather.3.cloned.1.call-update) | async-done | bytes 3145744 | tf_op jit(solution)/shard_map/all_gather | solution.py:152
  79.1 4.0 copy.145
  83.5 89.9 %while.26 = (s32[]{:T(128)}, f32[512,3,64]{0,2,1:T(8,128)S(1)}, bf16[4,1024,384]{1,2,0:T(8,128)(2,1)}, s32[512]{0:T(512)S(1)}, s32[4]{0:T(128)S(1)}, /*index=5*/...) while((s32[]{:T(128)}, f32[512,3,64]{0,2,1:T(8,128)S(1)}, ...), condition=%wide.region_6.7_spmd.clone, body=%wide.region_4.6_spmd.clone.sunk | while | flops 421229568 | bytes 9136299 | solution.py:67
  89.7 16.3 %fusion.364 = f32[512,3,64]{0,2,1:T(8,128)S(1)} fusion(bf16[1024,3,64]{0,2,1:T(8,128)(2,1)S(1)} %bitcast.400, f32[512,1024]{0,1:T(8,128)} %compare_convert_fusion.4, bf16[1024,3,64]{0,2,1:T(8,128)(2,1)S(1)} %bitcast.399, bf16[512,3,64]{0,2,1:T(8,128)(2,1)S(1)} %get-tuple-element.668, f32[512,3,64]{0,2,1:T(8,128)S(1)} %get-tuple-element.654, ...), kind=kOutput, calls=%fused_computation.16.clone.1 | convolution fusion | flops 420151296 | bytes 3866625 | tf_op jit(solution)/shard_map/while/body/eval_jaxpr/hbk,khe->bhe/dot_general | solution.py:147
  112.0 16.3 %fusion.364 = f32[512,3,64]{0,2,1:T(8,128)S(1)} fusion(bf16[1024,3,64]{0,2,1:T(8,128)(2,1)S(1)} %bitcast.400, f32[512,1024]{0,1:T(8,128)} %compare_convert_fusion.4, bf16[1024,3,64]{0,2,1:T(8,128)(2,1)S(1)} %bitcast.399, bf16[512,3,64]{0,2,1:T(8,128)(2,1)S(1)} %get-tuple-element.668, f32[512,3,64]{0,2,1:T(8,128)S(1)} %get-tuple-element.654, ...), kind=kOutput, calls=%fused_computation.16.clone.1 | convolution fusion | flops 420151296 | bytes 3866625 | tf_op jit(solution)/shard_map/while/body/eval_jaxpr/hbk,khe->bhe/dot_general | solution.py:147
  134.3 16.3 %fusion.364 = f32[512,3,64]{0,2,1:T(8,128)S(1)} fusion(bf16[1024,3,64]{0,2,1:T(8,128)(2,1)S(1)} %bitcast.400, f32[512,1024]{0,1:T(8,128)} %compare_convert_fusion.4, bf16[1024,3,64]{0,2,1:T(8,128)(2,1)S(1)} %bitcast.399, bf16[512,3,64]{0,2,1:T(8,128)(2,1)S(1)} %get-tuple-element.668, f32[512,3,64]{0,2,1:T(8,128)S(1)} %get-tuple-element.654, ...), kind=kOutput, calls=%fused_computation.16.clone.1 | convolution fusion | flops 420151296 | bytes 3866625 | tf_op jit(solution)/shard_map/while/body/eval_jaxpr/hbk,khe->bhe/dot_general | solution.py:147
  156.7 16.3 %fusion.364 = f32[512,3,64]{0,2,1:T(8,128)S(1)} fusion(bf16[1024,3,64]{0,2,1:T(8,128)(2,1)S(1)} %bitcast.400, f32[512,1024]{0,1:T(8,128)} %compare_convert_fusion.4, bf16[1024,3,64]{0,2,1:T(8,128)(2,1)S(1)} %bitcast.399, bf16[512,3,64]{0,2,1:T(8,128)(2,1)S(1)} %get-tuple-element.668, f32[512,3,64]{0,2,1:T(8,128)S(1)} %get-tuple-element.654, ...), kind=kOutput, calls=%fused_computation.16.clone.1 | convolution fusion | flops 420151296 | bytes 3866625 | tf_op jit(solution)/shard_map/while/body/eval_jaxpr/hbk,khe->bhe/dot_general | solution.py:147
  174.7 5.9 fusion.241
  183.0 41.1 %all-reduce.8.cloned.1.call-done = f32[512,768]{1,0:T(8,128)} async-done(((f32[512,768]{1,0:T(8,128)}), f32[512,768]{1,0:T(8,128)}) %all-reduce.8.cloned.1.call-update) | async-done | bytes 1572880 | tf_op jit(solution)/shard_map/psum | solution.py:169
  226.7 5.1 fusion.87
  234.7 43.0 %all-reduce.10.cloned.1.call-done = f32[512,768]{1,0:T(8,128)} async-done(((f32[512,768]{1,0:T(8,128)}), f32[512,768]{1,0:T(8,128)}) %all-reduce.10.cloned.1.call-update) | async-done | bytes 1572880 | tf_op jit(solution)/shard_map/psum | solution.py:175
  289.0 43.0 %all-reduce.12.cloned.1.call-done = f32[512,768]{1,0:T(8,128)} async-done(((f32[512,768]{1,0:T(8,128)}), f32[512,768]{1,0:T(8,128)}) %all-reduce.12.cloned.1.call-update) | async-done | bytes 1572880 | tf_op jit(solution)/shard_map/psum | solution.py:192
  350.2 3.8 collective-permute-done.3
  354.9 85.7 %all-gather.5.cloned.1.call-done = bf16[4096,768]{0,1:T(8,128)(2,1)} async-done(((bf16[512,768]{0,1:T(8,128)(2,1)}), bf16[4096,768]{0,1:T(8,128)(2,1)}) %all-gather.5.cloned.1.call-update) | async-done | bytes 6291472 | tf_op jit(solution)/shard_map/all_gather | solution.py:256
  440.7 6.4 copy.144
  447.1 304.2 %while.27 = (s32[]{:T(128)}, f32[512,3,64]{0,2,1:T(8,128)}, f32[512,3,64]{0,2,1:T(8,128)}, f32[512,3,64]{0,2,1:T(8,128)}, bf16[4,1024,768]{1,2,0:T(8,128)(2,1)},...) while((s32[]{:T(128)}, f32[512,3,64]{0,2,1:T(8,128)}, ...), condition=%wide.region_23.24_spmd.clone, body=%wide.region_21.23_spmd.clone.sunk | while | flops 1486976000 | bytes 64526712 | solution.py:67
  457.0 21.5 %fusion.382 = f32[512,3,64]{0,2,1:T(8,128)} fusion(bf16[1024,3,64]{0,2,1:T(8,128)(2,1)S(1)} %bitcast.393, f32[3,1024,512]{2,1,0:T(8,128)} %fusion.381, f32[1024,512]{1,0:T(8,128)S(1)} %compare_select_fusion.5, bf16[1024,3,64]{0,2,1:T(8,128)(2,1)} %bitcast.397, bf16[512,3,64]{0,2,1:T(8,128)(2,1)} %get-tuple-element.709, ...), kind=kOutput, calls=%fused_computation.66.clone.1 | convolution fusion | flops 431161344 | bytes 10158081 | tf_op jit(solution)/shard_map/while/body/eval_jaxpr/hbk,bhe->khe/dot_general | solution.py:245
  479.6 15.2 %fusion.383 = f32[512,3,64]{0,2,1:T(8,128)S(1)} fusion(bf16[1024,3,64]{0,2,1:T(8,128)(2,1)S(1)} %bitcast.398, f32[3,1024,512]{2,1,0:T(8,128)} %fusion.381, f32[1024,512]{1,0:T(8,128)S(1)} %compare_convert_fusion.5, f32[512,3,64]{0,2,1:T(8,128)S(1)} %copy-done.37, pred[]{:T(512)S(6)} %compare.7), kind=kOutput, calls=%fused_computation.65.clone.1 | convolution fusion | flops 218824704 | bytes 9568257 | tf_op jit(solution)/shard_map/while/body/eval_jaxpr/hbk,bhe->khe/dot_general | solution.py:248
  498.7 21.1 %fusion.380 = f32[512,3,64]{0,2,1:T(8,128)S(1)} fusion(bf16[1024,3,64]{0,2,1:T(8,128)(2,1)S(1)} %bitcast.396, f32[3,1024,512]{2,1,0:T(8,128)} %fusion.379, f32[512,1024]{0,1:T(8,128)S(1)} %compare_select_fusion.4, bf16[512,3,64]{0,2,1:T(8,128)(2,1)} %get-tuple-element.708, f32[512,3,64]{0,2,1:T(8,128)S(1)} %copy-done.40, pred[]{:T(512)S(6)} %compare.7), kind=kOutput, calls=%fused_computation.67.clone.1 | convolution fusion | flops 431161344 | bytes 9764865 | tf_op jit(solution)/shard_map/while/body/eval_jaxpr/hbk,khe->bhe/dot_general | solution.py:239
  531.1 21.3 %fusion.382 = f32[512,3,64]{0,2,1:T(8,128)} fusion(bf16[1024,3,64]{0,2,1:T(8,128)(2,1)S(1)} %bitcast.393, f32[3,1024,512]{2,1,0:T(8,128)} %fusion.381, f32[1024,512]{1,0:T(8,128)S(1)} %compare_select_fusion.5, bf16[1024,3,64]{0,2,1:T(8,128)(2,1)} %bitcast.397, bf16[512,3,64]{0,2,1:T(8,128)(2,1)} %get-tuple-element.709, ...), kind=kOutput, calls=%fused_computation.66.clone.1 | convolution fusion | flops 431161344 | bytes 10158081 | tf_op jit(solution)/shard_map/while/body/eval_jaxpr/hbk,bhe->khe/dot_general | solution.py:245
  553.5 15.2 %fusion.383 = f32[512,3,64]{0,2,1:T(8,128)S(1)} fusion(bf16[1024,3,64]{0,2,1:T(8,128)(2,1)S(1)} %bitcast.398, f32[3,1024,512]{2,1,0:T(8,128)} %fusion.381, f32[1024,512]{1,0:T(8,128)S(1)} %compare_convert_fusion.5, f32[512,3,64]{0,2,1:T(8,128)S(1)} %copy-done.37, pred[]{:T(512)S(6)} %compare.7), kind=kOutput, calls=%fused_computation.65.clone.1 | convolution fusion | flops 218824704 | bytes 9568257 | tf_op jit(solution)/shard_map/while/body/eval_jaxpr/hbk,bhe->khe/dot_general | solution.py:248
  572.6 21.3 %fusion.380 = f32[512,3,64]{0,2,1:T(8,128)S(1)} fusion(bf16[1024,3,64]{0,2,1:T(8,128)(2,1)S(1)} %bitcast.396, f32[3,1024,512]{2,1,0:T(8,128)} %fusion.379, f32[512,1024]{0,1:T(8,128)S(1)} %compare_select_fusion.4, bf16[512,3,64]{0,2,1:T(8,128)(2,1)} %get-tuple-element.708, f32[512,3,64]{0,2,1:T(8,128)S(1)} %copy-done.40, pred[]{:T(512)S(6)} %compare.7), kind=kOutput, calls=%fused_computation.67.clone.1 | convolution fusion | flops 431161344 | bytes 9764865 | tf_op jit(solution)/shard_map/while/body/eval_jaxpr/hbk,khe->bhe/dot_general | solution.py:239
  604.9 21.5 %fusion.382 = f32[512,3,64]{0,2,1:T(8,128)} fusion(bf16[1024,3,64]{0,2,1:T(8,128)(2,1)S(1)} %bitcast.393, f32[3,1024,512]{2,1,0:T(8,128)} %fusion.381, f32[1024,512]{1,0:T(8,128)S(1)} %compare_select_fusion.5, bf16[1024,3,64]{0,2,1:T(8,128)(2,1)} %bitcast.397, bf16[512,3,64]{0,2,1:T(8,128)(2,1)} %get-tuple-element.709, ...), kind=kOutput, calls=%fused_computation.66.clone.1 | convolution fusion | flops 431161344 | bytes 10158081 | tf_op jit(solution)/shard_map/while/body/eval_jaxpr/hbk,bhe->khe/dot_general | solution.py:245
  627.6 15.2 %fusion.383 = f32[512,3,64]{0,2,1:T(8,128)S(1)} fusion(bf16[1024,3,64]{0,2,1:T(8,128)(2,1)S(1)} %bitcast.398, f32[3,1024,512]{2,1,0:T(8,128)} %fusion.381, f32[1024,512]{1,0:T(8,128)S(1)} %compare_convert_fusion.5, f32[512,3,64]{0,2,1:T(8,128)S(1)} %copy-done.37, pred[]{:T(512)S(6)} %compare.7), kind=kOutput, calls=%fused_computation.65.clone.1 | convolution fusion | flops 218824704 | bytes 9568257 | tf_op jit(solution)/shard_map/while/body/eval_jaxpr/hbk,bhe->khe/dot_general | solution.py:248
  646.7 21.1 %fusion.380 = f32[512,3,64]{0,2,1:T(8,128)S(1)} fusion(bf16[1024,3,64]{0,2,1:T(8,128)(2,1)S(1)} %bitcast.396, f32[3,1024,512]{2,1,0:T(8,128)} %fusion.379, f32[512,1024]{0,1:T(8,128)S(1)} %compare_select_fusion.4, bf16[512,3,64]{0,2,1:T(8,128)(2,1)} %get-tuple-element.708, f32[512,3,64]{0,2,1:T(8,128)S(1)} %copy-done.40, pred[]{:T(512)S(6)} %compare.7), kind=kOutput, calls=%fused_computation.67.clone.1 | convolution fusion | flops 431161344 | bytes 9764865 | tf_op jit(solution)/shard_map/while/body/eval_jaxpr/hbk,khe->bhe/dot_general | solution.py:239
  679.1 21.3 %fusion.382 = f32[512,3,64]{0,2,1:T(8,128)} fusion(bf16[1024,3,64]{0,2,1:T(8,128)(2,1)S(1)} %bitcast.393, f32[3,1024,512]{2,1,0:T(8,128)} %fusion.381, f32[1024,512]{1,0:T(8,128)S(1)} %compare_select_fusion.5, bf16[1024,3,64]{0,2,1:T(8,128)(2,1)} %bitcast.397, bf16[512,3,64]{0,2,1:T(8,128)(2,1)} %get-tuple-element.709, ...), kind=kOutput, calls=%fused_computation.66.clone.1 | convolution fusion | flops 431161344 | bytes 10158081 | tf_op jit(solution)/shard_map/while/body/eval_jaxpr/hbk,bhe->khe/dot_general | solution.py:245
  701.5 15.2 %fusion.383 = f32[512,3,64]{0,2,1:T(8,128)S(1)} fusion(bf16[1024,3,64]{0,2,1:T(8,128)(2,1)S(1)} %bitcast.398, f32[3,1024,512]{2,1,0:T(8,128)} %fusion.381, f32[1024,512]{1,0:T(8,128)S(1)} %compare_convert_fusion.5, f32[512,3,64]{0,2,1:T(8,128)S(1)} %copy-done.37, pred[]{:T(512)S(6)} %compare.7), kind=kOutput, calls=%fused_computation.65.clone.1 | convolution fusion | flops 218824704 | bytes 9568257 | tf_op jit(solution)/shard_map/while/body/eval_jaxpr/hbk,bhe->khe/dot_general | solution.py:248
  720.6 21.3 %fusion.380 = f32[512,3,64]{0,2,1:T(8,128)S(1)} fusion(bf16[1024,3,64]{0,2,1:T(8,128)(2,1)S(1)} %bitcast.396, f32[3,1024,512]{2,1,0:T(8,128)} %fusion.379, f32[512,1024]{0,1:T(8,128)S(1)} %compare_select_fusion.4, bf16[512,3,64]{0,2,1:T(8,128)(2,1)} %get-tuple-element.708, f32[512,3,64]{0,2,1:T(8,128)S(1)} %copy-done.40, pred[]{:T(512)S(6)} %compare.7), kind=kOutput, calls=%fused_computation.67.clone.1 | convolution fusion | flops 431161344 | bytes 9764865 | tf_op jit(solution)/shard_map/while/body/eval_jaxpr/hbk,khe->bhe/dot_general | solution.py:239
  755.1 6.0 fusion.242
  783.4 34.6 %all-reduce = (bf16[2,192]{1,0:T(2,128)(2,1)S(1)}, bf16[3,33]{1,0:T(4,128)(2,1)S(1)}, bf16[768]{0:T(1024)(128)(2,1)S(1)}, bf16[768]{0:T(1024)(128)(2,1)S(1)}, bf...) all-reduce(bf16[2,192]{1,0:T(2,128)(2,1)S(1)} %pad_maximum_fusion.4, ...), channel_id=1, replica_groups=mesh['seq'=8,'mp'=4] {'seq'}, use_global_device_ids=true, to_apply=%region_29.30 | all-reduce | flops 5859 | bytes 23436 | tf_op jit(solution)/shard_map/psum | solution.py:282
  825.5 117.4 %all-reduce.16.cloned.1.call-done = (bf16[3,768,192]{1,2,0:T(8,128)(2,1)}, bf16[192,768]{1,0:T(8,128)(2,1)}, bf16[768,768]{1,0:T(8,128)(2,1)}, bf16[768,768]{1,0:T(8,128)(2,1)}) async-done(((bf16[3,768,192]{1,2,0:T(8,128)(2,1)}, bf16[192,768]{1,0:T(8,128)(2,1)}, bf16[768,768]{1,0:T(8,128)(2,1)}, bf16[768,768]{1,0:T(8,128)(2,1)}), (bf16[3,768,192]{1,2,0:T(8,128)(2,1)}, bf16[192,768]{1,0:T(8,128)(2,1)}, ...) | async-done | bytes 3538960 | tf_op jit(solution)/shard_map/psum | solution.py:281
  (721 shorter events, 177.5 us)
Async XLA Ops:
  7.2 219.2 %copy-start = (bf16[768,768]{1,0:T(8,128)(2,1)S(1)}, bf16[768,768]{1,0:T(8,128)(2,1)}, u32[]{:S(2)}) copy-start(bf16[768,768]{1,0:T(8,128)(2,1)} %param.29) | copy-start | bytes 3538948
  7.2 71.9 %all-gather.3.cloned.1.call-start = ((), (), s32[]{:S(2)}) async-start(), calls=%async_computation | async-start | bytes 3538944 | tf_op jit(solution)/shard_map/all_gather | solution.py:152
  11.2 328.3 %copy-start.46 = (f32[512,3]{0,1:T(4,128)}, f32[512,3]{0,1:T(4,128)S(1)}, u32[]{:S(2)}) copy-start(f32[512,3]{0,1:T(4,128)S(1)} %get-tuple-element.515) | copy-start | bytes 18436
  13.4 210.7 %all-reduce.8.cloned.1.call-start = ((), (), s32[]{:S(2)}) async-start(), calls=%async_computation.1 | async-start | bytes 3145728 | tf_op jit(solution)/shard_map/psum | solution.py:169
  14.3 12.2 %collective-permute-start = (bf16[16,192]{0,1:T(8,128)(2,1)S(1)}, bf16[16,192]{0,1:T(8,128)(2,1)S(1)}, u32[]{:S(2)}, u32[]{:S(2)}) collective-permute-start(bf16[16,192]{0,1:T(8,128)(2,1)S(1)} %get-tuple-element.438), channel_id=1, source_target_pairs={{0,4},{4,8},{8,12},{12,16},{16,20},{20,24},{24,28},{1,5},{5,9},{9,... | collective-permute-start | bytes 18440 | tf_op jit(solution)/shard_map/ppermute | solution.py:20
  19.2 7.4 collective-permute-start.1
  25.6 148.5 %copy-start.77 = (f32[512]{0:T(512)}, f32[512]{0:T(512)S(1)}, u32[]{:S(2)}) copy-start(f32[512]{0:T(512)S(1)} %get-tuple-element.492) | copy-start | bytes 6148
  25.6 148.5 %copy-start.80 = (f32[512]{0:T(512)}, f32[512]{0:T(512)S(1)}, u32[]{:S(2)}) copy-start(f32[512]{0:T(512)S(1)} %get-tuple-element.493) | copy-start | bytes 6148
  25.6 148.6 %copy-start.83 = (f32[512]{0:T(512)}, f32[512]{0:T(512)S(1)}, u32[]{:S(2)}) copy-start(f32[512]{0:T(512)S(1)} %get-tuple-element.494) | copy-start | bytes 6148
  25.6 148.6 %copy-start.86 = (f32[512]{0:T(512)}, f32[512]{0:T(512)S(1)}, u32[]{:S(2)}) copy-start(f32[512]{0:T(512)S(1)} %get-tuple-element.495) | copy-start | bytes 6148
  25.6 148.6 %copy-start.89 = (f32[512]{0:T(512)}, f32[512]{0:T(512)S(1)}, u32[]{:S(2)}) copy-start(f32[512]{0:T(512)S(1)} %get-tuple-element.496) | copy-start | bytes 6148
  25.6 148.6 %copy-start.92 = (f32[512]{0:T(512)}, f32[512]{0:T(512)S(1)}, u32[]{:S(2)}) copy-start(f32[512]{0:T(512)S(1)} %get-tuple-element.497) | copy-start | bytes 6148
  25.6 148.6 %copy-start.95 = (f32[512]{0:T(512)}, f32[512]{0:T(512)S(1)}, u32[]{:S(2)}) copy-start(f32[512]{0:T(512)S(1)} %get-tuple-element.498) | copy-start | bytes 6148
  25.6 148.6 %copy-start.98 = (f32[512]{0:T(512)}, f32[512]{0:T(512)S(1)}, u32[]{:S(2)}) copy-start(f32[512]{0:T(512)S(1)} %get-tuple-element.499) | copy-start | bytes 6148
  26.3 147.9 %copy-start.51 = (f32[512]{0:T(512)}, f32[512]{0:T(512)S(1)}, u32[]{:S(2)}) copy-start(f32[512]{0:T(512)S(1)} %get-tuple-element.475) | copy-start | bytes 6148
  26.3 147.9 %copy-start.53 = (f32[512]{0:T(512)}, f32[512]{0:T(512)S(1)}, u32[]{:S(2)}) copy-start(f32[512]{0:T(512)S(1)} %get-tuple-element.476) | copy-start | bytes 6148
  26.4 147.9 %copy-start.55 = (f32[512]{0:T(512)}, f32[512]{0:T(512)S(1)}, u32[]{:S(2)}) copy-start(f32[512]{0:T(512)S(1)} %get-tuple-element.483) | copy-start | bytes 6148
  26.4 147.9 %copy-start.57 = (f32[512]{0:T(512)}, f32[512]{0:T(512)S(1)}, u32[]{:S(2)}) copy-start(f32[512]{0:T(512)S(1)} %get-tuple-element.484) | copy-start | bytes 6148
  26.4 147.9 %copy-start.59 = (f32[512]{0:T(512)}, f32[512]{0:T(512)S(1)}, u32[]{:S(2)}) copy-start(f32[512]{0:T(512)S(1)} %get-tuple-element.485) | copy-start | bytes 6148
  26.4 147.9 %copy-start.62 = (f32[512]{0:T(512)}, f32[512]{0:T(512)S(1)}, u32[]{:S(2)}) copy-start(f32[512]{0:T(512)S(1)} %get-tuple-element.486) | copy-start | bytes 6148
  26.4 147.9 %copy-start.65 = (f32[512]{0:T(512)}, f32[512]{0:T(512)S(1)}, u32[]{:S(2)}) copy-start(f32[512]{0:T(512)S(1)} %get-tuple-element.487) | copy-start | bytes 6148
  26.4 147.9 %copy-start.68 = (f32[512]{0:T(512)}, f32[512]{0:T(512)S(1)}, u32[]{:S(2)}) copy-start(f32[512]{0:T(512)S(1)} %get-tuple-element.488) | copy-start | bytes 6148
  26.7 309.6 %copy-start.2 = (f32[544,192]{0,1:T(8,128)}, f32[544,192]{0,1:T(8,128)S(1)}, u32[]{:S(2)}) copy-start(f32[544,192]{0,1:T(8,128)S(1)} %maximum_convert_fusion) | copy-start | bytes 1253380
  182.9 94.8 %all-reduce.10.cloned.1.call-start = ((), (), s32[]{:S(2)}) async-start(), calls=%async_computation.2 | async-start | bytes 3145728 | tf_op jit(solution)/shard_map/psum | solution.py:175
  234.7 97.3 %all-reduce.12.cloned.1.call-start = ((), (), s32[]{:S(2)}) async-start(), calls=%async_computation.3 | async-start | bytes 3145728 | tf_op jit(solution)/shard_map/psum | solution.py:192
  288.9 151.7 %all-gather.5.cloned.1.call-start = ((), (), s32[]{:S(2)}) async-start(), calls=%async_computation.4 | async-start | bytes 7077888 | tf_op jit(solution)/shard_map/all_gather | solution.py:256
  339.4 483.9 %all-reduce.14.cloned.1.call-start = ((), (), s32[]{:S(2)}) async-start(), calls=%async_computation.5 | async-start | bytes 1572864 | tf_op jit(solution)/shard_map/psum | solution.py:278
  343.6 6.5 collective-permute-start.2
  347.0 7.0 collective-permute-start.3
  447.1 304.6 %copy-start.49 = (f32[512,3]{0,1:T(4,128)S(1)}, f32[512,3]{0,1:T(4,128)}, u32[]{:S(2)}) copy-start(f32[512,3]{0,1:T(4,128)} %copy-done.48) | copy-start | bytes 18436
  447.1 306.1 %copy-start.47 = (f32[512,3]{0,1:T(4,128)S(1)}, f32[512,3]{0,1:T(4,128)}, u32[]{:S(2)}) copy-start(f32[512,3]{0,1:T(4,128)} %copy-done.46) | copy-start | bytes 18436
  764.2 178.7 %all-reduce.16.cloned.1.call-start = ((), (), s32[]{:S(2)}) async-start(), calls=%async_computation.6 | async-start | bytes 7077888 | tf_op jit(solution)/shard_map/psum | solution.py:281
  (193 other events, 4999.3 us)
Sparse Core Ops, SparseCore 0:
  13.6 65.5 all-gather.2
  183.0 41.0 all-reduce.7
  234.8 42.8 all-reduce.9
  289.0 42.9 all-reduce.11
  339.6 101.0 all-gather.4
  764.3 32.8 all-reduce.13
  802.3 140.5 all-reduce.15
where the time goes:
time: 961 us; the launch traced here: 957 us
  waiting for transfers between devices  387 us (40%)
  matrix products  353 us (37%)
  other arithmetic  82.8 us (9%)
  local copies, waits for them, and re-layouts  59.3 us (6%)
  blocking collectives  34.6 us (4%)
  between operations  17.1 us (2%)
  loops' own time  12.2 us (1%)
  starting transfers between devices  11.1 us (1%)
    psum x1, waiting for transfers between devices, per_device(): lax.psum(d_w_qkv.astype(jnp.bfloat16), 'seq').astype(jnp.float32)  117 us
    all_gather x1, waiting for transfers between devices, per_device(): lax.all_gather(both_packed, 'seq', axis=0, tiled=True)  85.7 us
    dot_general x4, matrix products, pair_block(): jnp.einsum('hbk,bhe->khe', d_scores_own, queries_block, preferred_element...  85.6 us
    dot_general x4, matrix products, pair_block(): jnp.einsum('hbk,khe->bhe', d_scores, keys_block, preferred_element_type=j...  84.9 us
    dot_general x4, matrix products, attend(): jnp.einsum('hbk,khe->bhe', weights, values_heads, preferred_element_type=...  65.3 us
    dot_general x4, matrix products, pair_block(): jnp.einsum('hbk,bhe->khe', weights_own, d_attn_block, preferred_element_t...  60.7 us
    all_gather x1, waiting for transfers between devices, per_device(): lax.all_gather(packed, 'seq', axis=0, tiled=True)  52.4 us
    psum x1, waiting for transfers between devices, per_device(): d_first_out = d_second + lax.psum(d_first_part, 'mp')  43 us
  transfers between devices with their start and end apart: 11, of which 7 were waited for; matrix products, arithmetic and copies ran while one was open for 4% of the time, Pallas kernels for 0%

commit v1 on v0

--- a/solution.py
+++ b/solution.py
@@ -1,12 +1,31 @@
+import functools
 import math
 import jax
 import jax.numpy as jnp
 from jax import lax
 from jax.sharding import PartitionSpec as P
+from jax.lax import axis_index, axis_size, ppermute
 
 SHRINK = 0.95
 NORM_EPS = 1e-06
 LAYER_EPS = 1e-05
+
+
+def launch_widths(z, array_dim):
+    g_now = axis_size("seq")
+    right_arr, piece_now = (g_now, axis_index("seq"))
+    tmp, tall = (z, 1)
+    while tall < right_arr:
+        shaped = list(map(lambda ix: (ix, ix ^ tall), range(right_arr)))
+        mixed_arr = ppermute(tmp, "seq", shaped)
+        everything = jnp.concatenate([tmp, mixed_arr], array_dim)
+        carry_out = jnp.concatenate([mixed_arr, tmp], array_dim)
+        tmp = jnp.where(piece_now & tall == 0, everything, carry_out)
+        tall = 2 * tall
+    return tmp
+
+
+pair_the_rounds = functools.partial(launch_widths, array_dim=0)
 
 
 def padded(cells, sides, width):
@@ -252,10 +271,7 @@
 
     zero_state = (zero_heads, zero_heads, zero_heads)
     d_query, d_key_unit, d_value_heads = fold_blocks(
-        zero_state,
-        (lax.all_gather(both_packed, "seq", axis=0, tiled=True),),
-        jnp.int32(0),
-        pair_block,
+        zero_state, (pair_the_rounds(both_packed),), jnp.int32(0), pair_block
     )
     d_value_attn = d_value_heads.reshape(local_rows, columns)
     d_query_raw = query_scale * (

time: 961 us -> 1070 us (1.11)
  waiting for transfers between devices: 387 us -> 474 us
  other arithmetic: 82.8 us -> 105 us
    ppermute x0 -> x3, waiting for transfers between devices: none -> 172 us  [launch_widths(): mixed_arr = ppermute(tmp, 'seq', shaped)]
    all_gather x1 -> x0, waiting for transfers between devices: 85.7 us -> none  [per_device(): lax.all_gather(both_packed, 'seq', axis=0, tiled=True)]
    select_n x0 -> x3, other arithmetic: none -> 23.3 us  [launch_widths(): tmp = jnp.where(piece_now & tall == 0, everything, carry_out)]
  transfers between devices with their start and end apart: 11 -> 13, of which waited for: 7 -> 9; matrix products, arithmetic and copies ran while one was open for 4% -> 3% of each run, Pallas kernels for 0% -> 0%
where the time goes in v1:
time: 1070 us
  waiting for transfers between devices  474 us (44%)
  matrix products  353 us (33%)
  other arithmetic  105 us (10%)
  local copies, waits for them, and re-layouts  55.8 us (5%)
  blocking collectives  37.1 us (3%)
  starting transfers between devices  16.7 us (2%)
  between operations  16.5 us (2%)
  loops' own time  12.4 us (1%)
    ppermute x3, waiting for transfers between devices, launch_widths(): mixed_arr = ppermute(tmp, 'seq', shaped)  172 us
    psum x1, waiting for transfers between devices, per_device(): lax.psum(d_w_qkv.astype(jnp.bfloat16), 'seq').astype(jnp.float32)  118 us
    dot_general x4, matrix products, pair_block(): jnp.einsum('hbk,bhe->khe', d_scores_own, queries_block, preferred_element...  85.6 us
    dot_general x4, matrix products, pair_block(): jnp.einsum('hbk,khe->bhe', d_scores, keys_block, preferred_element_type=j...  84.9 us
    dot_general x4, matrix products, attend(): jnp.einsum('hbk,khe->bhe', weights, values_heads, preferred_element_type=...  65.3 us
    dot_general x4, matrix products, pair_block(): jnp.einsum('hbk,bhe->khe', weights_own, d_attn_block, preferred_element_t...  60.7 us
    all_gather x1, waiting for transfers between devices, per_device(): lax.all_gather(packed, 'seq', axis=0, tiled=True)  53.4 us
    psum x1, waiting for transfers between devices, per_device(): lax.psum(jnp.dot(act_low, w_down, preferred_element_type=jnp.float32), 'mp')  43 us
  transfers between devices with their start and end apart: 13, of which 9 were waited for; matrix products, arithmetic and copies ran while one was open for 3% of the time, Pallas kernels for 0%

profile of v1, /device:TPU:0, one launch (start us, length us, event | category | flops | bytes accessed | tf_op | source)
XLA Modules:
  0.0 1069.7 jit_solution(6018001746182230373)
XLA Ops:
  25.7 53.4 %all-gather.2.cloned.1.call-done = bf16[4096,384]{0,1:T(8,128)(2,1)} async-done(((bf16[512,384]{0,1:T(8,128)(2,1)}), bf16[4096,384]{0,1:T(8,128)(2,1)}) %all-gather.2.cloned.1.call-update) | async-done | bytes 3145744 | tf_op jit(solution)/shard_map/all_gather | solution.py:171
  83.1 90.0 %while.26 = (s32[]{:T(128)}, f32[512,3,64]{0,2,1:T(8,128)S(1)}, bf16[4,1024,384]{1,2,0:T(8,128)(2,1)}, s32[512]{0:T(512)S(1)}, s32[4]{0:T(128)S(1)}, /*index=5*/...) while((s32[]{:T(128)}, f32[512,3,64]{0,2,1:T(8,128)S(1)}, ...), condition=%wide.region_6.7_spmd.clone, body=%wide.region_4.6_spmd.clone.sunk | while | flops 421229568 | bytes 9136299 | solution.py:86
  89.6 16.3 %fusion.364 = f32[512,3,64]{0,2,1:T(8,128)S(1)} fusion(bf16[1024,3,64]{0,2,1:T(8,128)(2,1)S(1)} %bitcast.401, f32[512,1024]{0,1:T(8,128)} %compare_convert_fusion.4, bf16[1024,3,64]{0,2,1:T(8,128)(2,1)S(1)} %bitcast.400, bf16[512,3,64]{0,2,1:T(8,128)(2,1)S(1)} %get-tuple-element.668, f32[512,3,64]{0,2,1:T(8,128)S(1)} %get-tuple-element.654, ...), kind=kOutput, calls=%fused_computation.16.clone.1 | convolution fusion | flops 420151296 | bytes 3866625 | tf_op jit(solution)/shard_map/while/body/eval_jaxpr/hbk,khe->bhe/dot_general | solution.py:166
  111.9 16.3 %fusion.364 = f32[512,3,64]{0,2,1:T(8,128)S(1)} fusion(bf16[1024,3,64]{0,2,1:T(8,128)(2,1)S(1)} %bitcast.401, f32[512,1024]{0,1:T(8,128)} %compare_convert_fusion.4, bf16[1024,3,64]{0,2,1:T(8,128)(2,1)S(1)} %bitcast.400, bf16[512,3,64]{0,2,1:T(8,128)(2,1)S(1)} %get-tuple-element.668, f32[512,3,64]{0,2,1:T(8,128)S(1)} %get-tuple-element.654, ...), kind=kOutput, calls=%fused_computation.16.clone.1 | convolution fusion | flops 420151296 | bytes 3866625 | tf_op jit(solution)/shard_map/while/body/eval_jaxpr/hbk,khe->bhe/dot_general | solution.py:166
  134.3 16.3 %fusion.364 = f32[512,3,64]{0,2,1:T(8,128)S(1)} fusion(bf16[1024,3,64]{0,2,1:T(8,128)(2,1)S(1)} %bitcast.401, f32[512,1024]{0,1:T(8,128)} %compare_convert_fusion.4, bf16[1024,3,64]{0,2,1:T(8,128)(2,1)S(1)} %bitcast.400, bf16[512,3,64]{0,2,1:T(8,128)(2,1)S(1)} %get-tuple-element.668, f32[512,3,64]{0,2,1:T(8,128)S(1)} %get-tuple-element.654, ...), kind=kOutput, calls=%fused_computation.16.clone.1 | convolution fusion | flops 420151296 | bytes 3866625 | tf_op jit(solution)/shard_map/while/body/eval_jaxpr/hbk,khe->bhe/dot_general | solution.py:166
  156.6 16.3 %fusion.364 = f32[512,3,64]{0,2,1:T(8,128)S(1)} fusion(bf16[1024,3,64]{0,2,1:T(8,128)(2,1)S(1)} %bitcast.401, f32[512,1024]{0,1:T(8,128)} %compare_convert_fusion.4, bf16[1024,3,64]{0,2,1:T(8,128)(2,1)S(1)} %bitcast.400, bf16[512,3,64]{0,2,1:T(8,128)(2,1)S(1)} %get-tuple-element.668, f32[512,3,64]{0,2,1:T(8,128)S(1)} %get-tuple-element.654, ...), kind=kOutput, calls=%fused_computation.16.clone.1 | convolution fusion | flops 420151296 | bytes 3866625 | tf_op jit(solution)/shard_map/while/body/eval_jaxpr/hbk,khe->bhe/dot_general | solution.py:166
  174.1 6.2 fusion.241
  182.7 41.1 %all-reduce.8.cloned.1.call-done = f32[512,768]{1,0:T(8,128)} async-done(((f32[512,768]{1,0:T(8,128)}), f32[512,768]{1,0:T(8,128)}) %all-reduce.8.cloned.1.call-update) | async-done | bytes 1572880 | tf_op jit(solution)/shard_map/psum | solution.py:188
  234.4 43.0 %all-reduce.10.cloned.1.call-done = f32[512,768]{1,0:T(8,128)} async-done(((f32[512,768]{1,0:T(8,128)}), f32[512,768]{1,0:T(8,128)}) %all-reduce.10.cloned.1.call-update) | async-done | bytes 1572880 | tf_op jit(solution)/shard_map/psum | solution.py:194
  288.9 42.8 %all-reduce.12.cloned.1.call-done = f32[512,768]{1,0:T(8,128)} async-done(((f32[512,768]{1,0:T(8,128)}), f32[512,768]{1,0:T(8,128)}) %all-reduce.12.cloned.1.call-update) | async-done | bytes 1572880 | tf_op jit(solution)/shard_map/psum | solution.py:211
  341.9 18.0 %collective-permute-done.2 = bf16[512,768]{0,1:T(8,128)(2,1)} collective-permute-done((bf16[512,768]{0,1:T(8,128)(2,1)}, bf16[512,768]{0,1:T(8,128)(2,1)}, u32[]{:S(2)}, u32[]{:S(2)}) %collective-permute-start.2) | collective-permute-done | bytes 786464 | tf_op jit(solution)/shard_map/ppermute | solution.py:20
  359.9 10.8 %maximum_select_fusion.2 = bf16[1024,768]{0,1:T(8,128)(2,1)} fusion(bf16[512,768]{0,1:T(8,128)(2,1)} %collective-permute-done.2, bf16[512,192]{0,1:T(8,128)(2,1)S(1)} %bitcast.403, bf16[512,192]{0,1:T(8,128)(2,1)S(1)} %copy-done.22, bf16[512,192]{0,1:T(8,128)(2,1)S(1)} %copy-done.17, bf16[512,192]{0,1:T(8,128)(2,1)S(1)} %copy-done.21, pred[]{:T(512)S(6)} %eq.224), kind=kLoop, calls=%fused_computation.142 | loop fusion | flops 16515072 | bytes 3145729 | tf_op jit(solution)/shard_map/jit(_where)/select_n | solution.py:23
  372.2 33.9 %collective-permute-done.3 = bf16[1024,768]{0,1:T(8,128)(2,1)} collective-permute-done((bf16[1024,768]{0,1:T(8,128)(2,1)}, bf16[1024,768]{0,1:T(8,128)(2,1)}, u32[]{:S(2)}, u32[]{:S(2)}) %collective-permute-start.3) | collective-permute-done | bytes 1572896 | tf_op jit(solution)/shard_map/ppermute | solution.py:20
  406.1 5.2 maximum_select_fusion.1
  428.1 120.2 %collective-permute-done.4 = bf16[2048,768]{0,1:T(8,128)(2,1)} collective-permute-done((bf16[2048,768]{0,1:T(8,128)(2,1)}, bf16[2048,768]{0,1:T(8,128)(2,1)}, u32[]{:S(2)}, u32[]{:S(2)}) %collective-permute-start.4) | collective-permute-done | bytes 3145760 | tf_op jit(solution)/shard_map/ppermute | solution.py:20
  548.3 7.3 maximum_select_fusion
  559.0 303.2 %while.27 = (s32[]{:T(128)}, f32[512,3,64]{0,2,1:T(8,128)}, f32[512,3,64]{0,2,1:T(8,128)}, f32[512,3,64]{0,2,1:T(8,128)}, bf16[4,1024,768]{1,2,0:T(8,128)(2,1)},...) while((s32[]{:T(128)}, f32[512,3,64]{0,2,1:T(8,128)}, ...), condition=%wide.region_23.24_spmd.clone, body=%wide.region_21.23_spmd.clone.sunk | while | flops 1486976000 | bytes 64526712 | solution.py:86
  568.9 21.3 %fusion.382 = f32[512,3,64]{0,2,1:T(8,128)} fusion(bf16[1024,3,64]{0,2,1:T(8,128)(2,1)S(1)} %bitcast.393, f32[3,1024,512]{2,1,0:T(8,128)} %fusion.381, f32[1024,512]{1,0:T(8,128)S(1)} %compare_select_fusion.5, bf16[1024,3,64]{0,2,1:T(8,128)(2,1)} %bitcast.398, bf16[512,3,64]{0,2,1:T(8,128)(2,1)} %get-tuple-element.709, ...), kind=kOutput, calls=%fused_computation.66.clone.1 | convolution fusion | flops 431161344 | bytes 10158081 | tf_op jit(solution)/shard_map/while/body/eval_jaxpr/hbk,bhe->khe/dot_general | solution.py:264
  591.3 15.2 %fusion.383 = f32[512,3,64]{0,2,1:T(8,128)S(1)} fusion(bf16[1024,3,64]{0,2,1:T(8,128)(2,1)S(1)} %bitcast.399, f32[3,1024,512]{2,1,0:T(8,128)} %fusion.381, f32[1024,512]{1,0:T(8,128)S(1)} %compare_convert_fusion.5, f32[512,3,64]{0,2,1:T(8,128)S(1)} %copy-done.37, pred[]{:T(512)S(6)} %compare.7), kind=kOutput, calls=%fused_computation.65.clone.1 | convolution fusion | flops 218824704 | bytes 9568257 | tf_op jit(solution)/shard_map/while/body/eval_jaxpr/hbk,bhe->khe/dot_general | solution.py:267
  610.4 21.3 %fusion.380 = f32[512,3,64]{0,2,1:T(8,128)S(1)} fusion(bf16[1024,3,64]{0,2,1:T(8,128)(2,1)S(1)} %bitcast.397, f32[3,1024,512]{2,1,0:T(8,128)} %fusion.379, f32[512,1024]{0,1:T(8,128)S(1)} %compare_select_fusion.4, bf16[512,3,64]{0,2,1:T(8,128)(2,1)} %get-tuple-element.708, f32[512,3,64]{0,2,1:T(8,128)S(1)} %copy-done.40, pred[]{:T(512)S(6)} %compare.7), kind=kOutput, calls=%fused_computation.67.clone.1 | convolution fusion | flops 431161344 | bytes 9764865 | tf_op jit(solution)/shard_map/while/body/eval_jaxpr/hbk,khe->bhe/dot_general | solution.py:258
  642.4 21.5 %fusion.382 = f32[512,3,64]{0,2,1:T(8,128)} fusion(bf16[1024,3,64]{0,2,1:T(8,128)(2,1)S(1)} %bitcast.393, f32[3,1024,512]{2,1,0:T(8,128)} %fusion.381, f32[1024,512]{1,0:T(8,128)S(1)} %compare_select_fusion.5, bf16[1024,3,64]{0,2,1:T(8,128)(2,1)} %bitcast.398, bf16[512,3,64]{0,2,1:T(8,128)(2,1)} %get-tuple-element.709, ...), kind=kOutput, calls=%fused_computation.66.clone.1 | convolution fusion | flops 431161344 | bytes 10158081 | tf_op jit(solution)/shard_map/while/body/eval_jaxpr/hbk,bhe->khe/dot_general | solution.py:264
  665.1 15.2 %fusion.383 = f32[512,3,64]{0,2,1:T(8,128)S(1)} fusion(bf16[1024,3,64]{0,2,1:T(8,128)(2,1)S(1)} %bitcast.399, f32[3,1024,512]{2,1,0:T(8,128)} %fusion.381, f32[1024,512]{1,0:T(8,128)S(1)} %compare_convert_fusion.5, f32[512,3,64]{0,2,1:T(8,128)S(1)} %copy-done.37, pred[]{:T(512)S(6)} %compare.7), kind=kOutput, calls=%fused_computation.65.clone.1 | convolution fusion | flops 218824704 | bytes 9568257 | tf_op jit(solution)/shard_map/while/body/eval_jaxpr/hbk,bhe->khe/dot_general | solution.py:267
  684.2 21.1 %fusion.380 = f32[512,3,64]{0,2,1:T(8,128)S(1)} fusion(bf16[1024,3,64]{0,2,1:T(8,128)(2,1)S(1)} %bitcast.397, f32[3,1024,512]{2,1,0:T(8,128)} %fusion.379, f32[512,1024]{0,1:T(8,128)S(1)} %compare_select_fusion.4, bf16[512,3,64]{0,2,1:T(8,128)(2,1)} %get-tuple-element.708, f32[512,3,64]{0,2,1:T(8,128)S(1)} %copy-done.40, pred[]{:T(512)S(6)} %compare.7), kind=kOutput, calls=%fused_computation.67.clone.1 | convolution fusion | flops 431161344 | bytes 9764865 | tf_op jit(solution)/shard_map/while/body/eval_jaxpr/hbk,khe->bhe/dot_general | solution.py:258
  716.3 21.3 %fusion.382 = f32[512,3,64]{0,2,1:T(8,128)} fusion(bf16[1024,3,64]{0,2,1:T(8,128)(2,1)S(1)} %bitcast.393, f32[3,1024,512]{2,1,0:T(8,128)} %fusion.381, f32[1024,512]{1,0:T(8,128)S(1)} %compare_select_fusion.5, bf16[1024,3,64]{0,2,1:T(8,128)(2,1)} %bitcast.398, bf16[512,3,64]{0,2,1:T(8,128)(2,1)} %get-tuple-element.709, ...), kind=kOutput, calls=%fused_computation.66.clone.1 | convolution fusion | flops 431161344 | bytes 10158081 | tf_op jit(solution)/shard_map/while/body/eval_jaxpr/hbk,bhe->khe/dot_general | solution.py:264
  738.7 15.2 %fusion.383 = f32[512,3,64]{0,2,1:T(8,128)S(1)} fusion(bf16[1024,3,64]{0,2,1:T(8,128)(2,1)S(1)} %bitcast.399, f32[3,1024,512]{2,1,0:T(8,128)} %fusion.381, f32[1024,512]{1,0:T(8,128)S(1)} %compare_convert_fusion.5, f32[512,3,64]{0,2,1:T(8,128)S(1)} %copy-done.37, pred[]{:T(512)S(6)} %compare.7), kind=kOutput, calls=%fused_computation.65.clone.1 | convolution fusion | flops 218824704 | bytes 9568257 | tf_op jit(solution)/shard_map/while/body/eval_jaxpr/hbk,bhe->khe/dot_general | solution.py:267
  757.8 21.3 %fusion.380 = f32[512,3,64]{0,2,1:T(8,128)S(1)} fusion(bf16[1024,3,64]{0,2,1:T(8,128)(2,1)S(1)} %bitcast.397, f32[3,1024,512]{2,1,0:T(8,128)} %fusion.379, f32[512,1024]{0,1:T(8,128)S(1)} %compare_select_fusion.4, bf16[512,3,64]{0,2,1:T(8,128)(2,1)} %get-tuple-element.708, f32[512,3,64]{0,2,1:T(8,128)S(1)} %copy-done.40, pred[]{:T(512)S(6)} %compare.7), kind=kOutput, calls=%fused_computation.67.clone.1 | convolution fusion | flops 431161344 | bytes 9764865 | tf_op jit(solution)/shard_map/while/body/eval_jaxpr/hbk,khe->bhe/dot_general | solution.py:258
  789.9 21.5 %fusion.382 = f32[512,3,64]{0,2,1:T(8,128)} fusion(bf16[1024,3,64]{0,2,1:T(8,128)(2,1)S(1)} %bitcast.393, f32[3,1024,512]{2,1,0:T(8,128)} %fusion.381, f32[1024,512]{1,0:T(8,128)S(1)} %compare_select_fusion.5, bf16[1024,3,64]{0,2,1:T(8,128)(2,1)} %bitcast.398, bf16[512,3,64]{0,2,1:T(8,128)(2,1)} %get-tuple-element.709, ...), kind=kOutput, calls=%fused_computation.66.clone.1 | convolution fusion | flops 431161344 | bytes 10158081 | tf_op jit(solution)/shard_map/while/body/eval_jaxpr/hbk,bhe->khe/dot_general | solution.py:264
  812.5 15.2 %fusion.383 = f32[512,3,64]{0,2,1:T(8,128)S(1)} fusion(bf16[1024,3,64]{0,2,1:T(8,128)(2,1)S(1)} %bitcast.399, f32[3,1024,512]{2,1,0:T(8,128)} %fusion.381, f32[1024,512]{1,0:T(8,128)S(1)} %compare_convert_fusion.5, f32[512,3,64]{0,2,1:T(8,128)S(1)} %copy-done.37, pred[]{:T(512)S(6)} %compare.7), kind=kOutput, calls=%fused_computation.65.clone.1 | convolution fusion | flops 218824704 | bytes 9568257 | tf_op jit(solution)/shard_map/while/body/eval_jaxpr/hbk,bhe->khe/dot_general | solution.py:267
  831.6 21.1 %fusion.380 = f32[512,3,64]{0,2,1:T(8,128)S(1)} fusion(bf16[1024,3,64]{0,2,1:T(8,128)(2,1)S(1)} %bitcast.397, f32[3,1024,512]{2,1,0:T(8,128)} %fusion.379, f32[512,1024]{0,1:T(8,128)S(1)} %compare_select_fusion.4, bf16[512,3,64]{0,2,1:T(8,128)(2,1)} %get-tuple-element.708, f32[512,3,64]{0,2,1:T(8,128)S(1)} %copy-done.40, pred[]{:T(512)S(6)} %compare.7), kind=kOutput, calls=%fused_computation.67.clone.1 | convolution fusion | flops 431161344 | bytes 9764865 | tf_op jit(solution)/shard_map/while/body/eval_jaxpr/hbk,khe->bhe/dot_general | solution.py:258
  866.0 6.2 fusion.242
  893.1 37.1 %all-reduce = (bf16[2,192]{1,0:T(2,128)(2,1)S(1)}, bf16[3,33]{1,0:T(4,128)(2,1)S(1)}, bf16[768]{0:T(1024)(128)(2,1)S(1)}, bf16[768]{0:T(1024)(128)(2,1)S(1)}, bf...) all-reduce(bf16[2,192]{1,0:T(2,128)(2,1)S(1)} %pad_maximum_fusion.4, ...), channel_id=1, replica_groups=mesh['seq'=8,'mp'=4] {'seq'}, use_global_device_ids=true, to_apply=%region_29.30 | all-reduce | flops 5859 | bytes 23436 | tf_op jit(solution)/shard_map/psum | solution.py:298
  937.7 118.2 %all-reduce.16.cloned.1.call-done = (bf16[3,768,192]{1,2,0:T(8,128)(2,1)}, bf16[192,768]{1,0:T(8,128)(2,1)}, bf16[768,768]{1,0:T(8,128)(2,1)}, bf16[768,768]{1,0:T(8,128)(2,1)}) async-done(((bf16[3,768,192]{1,2,0:T(8,128)(2,1)}, bf16[192,768]{1,0:T(8,128)(2,1)}, bf16[768,768]{1,0:T(8,128)(2,1)}, bf16[768,768]{1,0:T(8,128)(2,1)}), (bf16[3,768,192]{1,2,0:T(8,128)(2,1)}, bf16[192,768]{1,0:T(8,128)(2,1)}, ...) | async-done | bytes 3538960 | tf_op jit(solution)/shard_map/psum | solution.py:297
  (661 shorter events, 200.6 us)
Async XLA Ops:
  7.2 218.9 %copy-start = (bf16[768,768]{1,0:T(8,128)(2,1)S(1)}, bf16[768,768]{1,0:T(8,128)(2,1)}, u32[]{:S(2)}) copy-start(bf16[768,768]{1,0:T(8,128)(2,1)} %param.29) | copy-start | bytes 3538948
  7.2 72.0 %all-gather.2.cloned.1.call-start = ((), (), s32[]{:S(2)}) async-start(), calls=%async_computation | async-start | bytes 3538944 | tf_op jit(solution)/shard_map/all_gather | solution.py:171
  11.2 402.5 %copy-start.46 = (f32[512,3]{0,1:T(4,128)}, f32[512,3]{0,1:T(4,128)S(1)}, u32[]{:S(2)}) copy-start(f32[512,3]{0,1:T(4,128)S(1)} %get-tuple-element.515) | copy-start | bytes 18436
  13.4 210.4 %all-reduce.8.cloned.1.call-start = ((), (), s32[]{:S(2)}) async-start(), calls=%async_computation.1 | async-start | bytes 3145728 | tf_op jit(solution)/shard_map/psum | solution.py:188
  14.3 11.2 %collective-permute-start = (bf16[16,192]{0,1:T(8,128)(2,1)S(1)}, bf16[16,192]{0,1:T(8,128)(2,1)S(1)}, u32[]{:S(2)}, u32[]{:S(2)}) collective-permute-start(bf16[16,192]{0,1:T(8,128)(2,1)S(1)} %get-tuple-element.438), channel_id=1, source_target_pairs={{0,4},{4,8},{8,12},{12,16},{16,20},{20,24},{24,28},{1,5},{5,9},{9,... | collective-permute-start | bytes 18440 | tf_op jit(solution)/shard_map/ppermute | solution.py:39
  19.2 6.3 collective-permute-start.1
  23.1 313.0 %copy-start.123 = (f32[512]{0:T(512)}, f32[512]{0:T(512)S(1)}, u32[]{:S(2)}) copy-start(f32[512]{0:T(512)S(1)} %get-tuple-element.423) | copy-start | bytes 6148
  23.7 150.1 %copy-start.128 = (f32[1,192]{1,0:T(1,128)}, f32[1,192]{1,0:T(1,128)S(1)}, u32[]{:S(2)}) copy-start(f32[1,192]{1,0:T(1,128)S(1)} %get-tuple-element.459) | copy-start | bytes 2308
  23.7 150.1 %copy-start.130 = (f32[1,192]{1,0:T(1,128)}, f32[1,192]{1,0:T(1,128)S(1)}, u32[]{:S(2)}) copy-start(f32[1,192]{1,0:T(1,128)S(1)} %get-tuple-element.460) | copy-start | bytes 2308
  23.7 150.1 %copy-start.132 = (f32[1,192]{1,0:T(1,128)}, f32[1,192]{1,0:T(1,128)S(1)}, u32[]{:S(2)}) copy-start(f32[1,192]{1,0:T(1,128)S(1)} %get-tuple-element.461) | copy-start | bytes 2308
  23.7 150.1 %copy-start.134 = (f32[1,192]{1,0:T(1,128)}, f32[1,192]{1,0:T(1,128)S(1)}, u32[]{:S(2)}) copy-start(f32[1,192]{1,0:T(1,128)S(1)} %get-tuple-element.462) | copy-start | bytes 2308
  25.1 148.8 %copy-start.83 = (f32[512]{0:T(512)}, f32[512]{0:T(512)S(1)}, u32[]{:S(2)}) copy-start(f32[512]{0:T(512)S(1)} %get-tuple-element.494) | copy-start | bytes 6148
  25.1 148.8 %copy-start.86 = (f32[512]{0:T(512)}, f32[512]{0:T(512)S(1)}, u32[]{:S(2)}) copy-start(f32[512]{0:T(512)S(1)} %get-tuple-element.495) | copy-start | bytes 6148
  25.1 148.8 %copy-start.89 = (f32[512]{0:T(512)}, f32[512]{0:T(512)S(1)}, u32[]{:S(2)}) copy-start(f32[512]{0:T(512)S(1)} %get-tuple-element.496) | copy-start | bytes 6148
  25.1 148.8 %copy-start.92 = (f32[512]{0:T(512)}, f32[512]{0:T(512)S(1)}, u32[]{:S(2)}) copy-start(f32[512]{0:T(512)S(1)} %get-tuple-element.497) | copy-start | bytes 6148
  25.1 148.8 %copy-start.95 = (f32[512]{0:T(512)}, f32[512]{0:T(512)S(1)}, u32[]{:S(2)}) copy-start(f32[512]{0:T(512)S(1)} %get-tuple-element.498) | copy-start | bytes 6148
  25.1 148.8 %copy-start.98 = (f32[512]{0:T(512)}, f32[512]{0:T(512)S(1)}, u32[]{:S(2)}) copy-start(f32[512]{0:T(512)S(1)} %get-tuple-element.499) | copy-start | bytes 6148
  25.1 311.0 %copy-start.125 = (f32[512]{0:T(512)}, f32[512]{0:T(512)S(1)}, u32[]{:S(2)}) copy-start(f32[512]{0:T(512)S(1)} %get-tuple-element.491) | copy-start | bytes 6148
  25.4 310.7 %copy-start.119 = (f32[512]{0:T(512)}, f32[512]{0:T(512)S(1)}, u32[]{:S(2)}) copy-start(f32[512]{0:T(512)S(1)} %get-tuple-element.473) | copy-start | bytes 6148
  25.4 310.7 %copy-start.121 = (f32[512]{0:T(512)}, f32[512]{0:T(512)S(1)}, u32[]{:S(2)}) copy-start(f32[512]{0:T(512)S(1)} %get-tuple-element.474) | copy-start | bytes 6148
  25.7 310.4 %copy-start.2 = (f32[544,192]{0,1:T(8,128)}, f32[544,192]{0,1:T(8,128)S(1)}, u32[]{:S(2)}) copy-start(f32[544,192]{0,1:T(8,128)S(1)} %maximum_convert_fusion) | copy-start | bytes 1253380
  182.6 94.8 %all-reduce.10.cloned.1.call-start = ((), (), s32[]{:S(2)}) async-start(), calls=%async_computation.2 | async-start | bytes 3145728 | tf_op jit(solution)/shard_map/psum | solution.py:194
  234.4 97.3 %all-reduce.12.cloned.1.call-start = ((), (), s32[]{:S(2)}) async-start(), calls=%async_computation.3 | async-start | bytes 3145728 | tf_op jit(solution)/shard_map/psum | solution.py:211
  288.6 646.9 %all-reduce.14.cloned.1.call-start = ((), (), s32[]{:S(2)}) async-start(), calls=%async_computation.4 | async-start | bytes 1572864 | tf_op jit(solution)/shard_map/psum | solution.py:294
  340.4 19.5 %collective-permute-start.2 = (bf16[512,768]{0,1:T(8,128)(2,1)}, bf16[512,768]{0,1:T(8,128)(2,1)}, u32[]{:S(2)}, u32[]{:S(2)}) collective-permute-start(bf16[512,768]{0,1:T(8,128)(2,1)} %pad_maximum_fusion), channel_id=1, source_target_pairs={{0,4},{4,0},{8,12},{12,8},{16,20},{20,16},{24,28},{28,24},{1,5},{5... | collective-permute-start | bytes 2359304 | tf_op jit(solution)/shard_map/ppermute | solution.py:20
  370.7 35.4 %collective-permute-start.3 = (bf16[1024,768]{0,1:T(8,128)(2,1)}, bf16[1024,768]{0,1:T(8,128)(2,1)}, u32[]{:S(2)}, u32[]{:S(2)}) collective-permute-start(bf16[1024,768]{0,1:T(8,128)(2,1)} %maximum_select_fusion.2), channel_id=1, source_target_pairs={{0,8},{4,12},{8,0},{12,4},{16,24},{20,28},{24,16},{28,20},{1,9},{5... | collective-permute-start | bytes 4718600 | tf_op jit(solution)/shard_map/ppermute | solution.py:20
  411.3 137.0 %collective-permute-start.4 = (bf16[2048,768]{0,1:T(8,128)(2,1)}, bf16[2048,768]{0,1:T(8,128)(2,1)}, u32[]{:S(2)}, u32[]{:S(2)}) collective-permute-start(bf16[2048,768]{0,1:T(8,128)(2,1)} %maximum_select_fusion.1), channel_id=1, source_target_pairs={{0,16},{4,20},{8,24},{12,28},{16,0},{20,4},{24,8},{28,12},{1,17},{... | collective-permute-start | bytes 9437192 | tf_op jit(solution)/shard_map/ppermute | solution.py:20
  417.8 6.5 collective-permute-start.5
  421.2 6.0 collective-permute-start.6
  559.0 303.5 %copy-start.49 = (f32[512,3]{0,1:T(4,128)S(1)}, f32[512,3]{0,1:T(4,128)}, u32[]{:S(2)}) copy-start(f32[512,3]{0,1:T(4,128)} %copy-done.48) | copy-start | bytes 18436
  559.0 305.1 %copy-start.47 = (f32[512,3]{0,1:T(4,128)S(1)}, f32[512,3]{0,1:T(4,128)}, u32[]{:S(2)}) copy-start(f32[512,3]{0,1:T(4,128)} %copy-done.46) | copy-start | bytes 18436
  874.0 181.9 %all-reduce.16.cloned.1.call-start = ((), (), s32[]{:S(2)}) async-start(), calls=%async_computation.5 | async-start | bytes 7077888 | tf_op jit(solution)/shard_map/psum | solution.py:297
  (162 other events, 3412.4 us)
Sparse Core Ops, SparseCore 0:
  13.6 65.5 all-gather.1
  182.7 41.0 all-reduce.7
  234.5 42.8 all-reduce.9
  288.7 42.8 all-reduce.11
  874.1 36.1 all-reduce.13
  915.3 140.5 all-reduce.15
